TPU v7x, 32 devices: a whole 2x2x4 slice. The times are simulated.
32 devices in a mesh: tm: 8 (over z, x), chan: 4 (over y, core).
Axes of the slice: x: 2, y: 2, z: 4, core: 2. Of those that a mesh axis runs over, the one named last changes fastest.
Arguments:
- record: float32 [8192, 1024], P('tm', 'chan'), may hold values from -120 to 120
- test_matrix: float32 [64, 1024, 128], P(None, 'chan'), may hold values from -0.0234375 to 0.0234375
Outputs:
- basis: float32 [8192, 128], P('tm')
- coeffs: float32 [64, 1024, 128], P('tm', 'chan')
All inputs are finite; a program needn't handle non-finite values.
Results may differ from a plain program's by a relative error of at most 0.00024.
Values sent between devices are 32-bit elements; how exact they have to be, the bound alone decides.
No kernel may reach another device: no remote copies, remote signals or barrier semaphores. Data moves between devices by JAX's collectives and lax.ppermute only.
A program may use at most 256 MiB of HBM per device.

v0:
```python
import math
import jax
import jax.numpy as jnp
from jax import lax
from jax.sharding import PartitionSpec as P

L = 64


def passed_along(block, axis, distance):
    devices = range(lax.axis_size(axis))
    route = [(i - distance, i) for i in devices if i - distance in devices]
    return lax.ppermute(block, axis, route)


def sketch_part(extended, test_local, rows):
    hi = lax.Precision.HIGHEST
    chans = test_local.shape[1]
    width = test_local.shape[2]
    total = jnp.zeros((rows, width), jnp.float32)
    for group in range(L // 8):
        block = jnp.concatenate(
            [extended[group * 8 + j : group * 8 + j + rows] for j in range(8)], axis=1
        )
        weights = test_local[group * 8 : (group + 1) * 8].reshape(8 * chans, width)
        total = total + jnp.dot(block, weights, precision=hi, preferred_element_type=jnp.float32)
    return total


def on_device(record, test_matrix):
    hi = lax.Precision.HIGHEST
    rows = record.shape[0]
    chans = record.shape[1]
    width = test_matrix.shape[2]
    n_time = lax.axis_size("tm")
    total_rows = rows * n_time
    rim = passed_along(record[: L - 1], "tm", -1)
    extended = jnp.concatenate([record, rim], axis=0)
    partial_value = sketch_part(extended, test_matrix, rows)
    own = lax.psum_scatter(partial_value, "chan", scatter_dimension=0, tiled=True)
    gram = jnp.dot(own.T, own, precision=hi, preferred_element_type=jnp.float32)
    lower = jnp.linalg.cholesky(lax.psum(gram, ("tm", "chan")))
    root = jnp.sqrt(jnp.float32(total_rows))
    share = (
        lax.linalg.triangular_solve(lower, own, left_side=False, lower=True, transpose_a=True)
        * root
    )
    basis = lax.all_gather(share, "chan", axis=0, tiled=True)
    scale = 1.0 / root
    start = jnp.int32(0)
    group = math.gcd(lax.axis_size("tm") * (L // n_time), 8)
    pieces = []
    for first in range(0, lax.axis_size("tm") * (L // n_time), group):
        block = jnp.concatenate(
            [lax.dynamic_slice_in_dim(extended, start + first + j, rows, 0) for j in range(group)],
            axis=1,
        )
        term = lax.dot_general(
            block, basis, (((0,), (0,)), ((), ())), precision=hi, preferred_element_type=jnp.float32
        )
        pieces.append(term.reshape(group, chans, width))
    coeffs = lax.psum_scatter(
        jnp.concatenate(pieces, axis=0) * scale, "tm", scatter_dimension=0, tiled=True
    )
    return (basis, coeffs)


def solution(mesh):
    placed = (P("tm", "chan"), P(None, "chan", None))
    return jax.shard_map(
        on_device,
        mesh=mesh,
        in_specs=placed,
        out_specs=(P("tm", None), P("tm", "chan", None)),
        check_vma=False,
    )
```

profile of v0, /device:TPU:0, one launch (start us, length us, event | category | flops | bytes accessed | tf_op | source)
XLA Modules:
  0.0 572.7 jit_solution(13978210390161302283)
XLA Ops:
  7.2 0.0 reduce-scatter.3.cloned.1.call-start
  7.2 0.8 slice.226
  8.1 1.4 collective-permute-start
  9.5 5.8 %fusion.9 = (f32[8,256,128]{2,1,0:T(8,128)}, f32[8,256,128]{2,1,0:T(8,128)S(1)}, f32[8,256,128]{2,1,0:T(8,128)S(1)}, f32[8,256,128]{2,1,0:T(8,128)}, f32[8,256,1...) fusion(f32[64,256,128]{2,1,0:T(8,128)} %param.3), kind=kLoop, calls=%fused_computation.92 | loop fusion | bytes 16777216 | tf_op jit(solution)/shard_map/slice | solution.py:25
  15.3 1.2 constant_dynamic-update-slice_fusion.2
  16.5 0.0 collective-permute-done
  16.5 2.5 slice_dynamic-update-slice_fusion.55
  19.0 2.8 slice_dynamic-update-slice_fusion.62
  21.8 2.7 slice_dynamic-update-slice_fusion.61
  24.5 2.7 slice_dynamic-update-slice_fusion.60
  27.2 2.8 slice_dynamic-update-slice_fusion.59
  30.0 2.8 slice_dynamic-update-slice_fusion.58
  32.8 2.9 slice_dynamic-update-slice_fusion.57
  35.7 2.9 slice_dynamic-update-slice_fusion.56
  38.6 19.3 %fusion.10 = f32[1024,128]{1,0:T(8,128)S(1)} fusion(f32[1024,2048]{1,0:T(8,128)S(1)} %get-tuple-element.17, f32[2048,128]{1,0:T(8,128)} %bitcast.94), kind=kOutput, calls=%fused_computation.93 | convolution fusion | flops 3221225472 | bytes 9961472 | tf_op jit(solution)/shard_map/dot_general | solution.py:26
  58.0 0.0 slice-start.6
  58.0 9.2 %fusion.11 = f32[1024,128]{1,0:T(8,128)S(1)} fusion(f32[1024,2048]{1,0:T(8,128)} %get-tuple-element.16, f32[2048,128]{1,0:T(8,128)S(1)} %bitcast.93), kind=kOutput, calls=%fused_computation.94 | convolution fusion | flops 3221225472 | bytes 9961472 | tf_op jit(solution)/shard_map/dot_general | solution.py:26
  67.2 0.0 slice-start.7
  67.2 6.7 %fusion.12 = f32[1024,128]{1,0:T(8,128)S(1)} fusion(f32[1024,2048]{1,0:T(8,128)S(1)} %copy-done.2, f32[2048,128]{1,0:T(8,128)S(1)} %bitcast.92), kind=kOutput, calls=%fused_computation.95 | convolution fusion | flops 3221225472 | bytes 9961472 | tf_op jit(solution)/shard_map/dot_general | solution.py:26
  73.9 0.0 slice-start.2
  73.9 9.6 %fusion.13 = f32[1024,128]{1,0:T(8,128)S(1)} fusion(f32[1024,2048]{1,0:T(8,128)} %get-tuple-element.14, f32[2048,128]{1,0:T(8,128)S(1)} %bitcast.91), kind=kOutput, calls=%fused_computation.96 | convolution fusion | flops 3221225472 | bytes 9961472 | tf_op jit(solution)/shard_map/dot_general | solution.py:26
  83.6 0.0 slice-start.3
  83.6 6.7 %fusion.14 = f32[1024,128]{1,0:T(8,128)S(1)} fusion(f32[1024,2048]{1,0:T(8,128)S(1)} %bitcast.67, f32[2048,128]{1,0:T(8,128)S(1)} %bitcast.90), kind=kOutput, calls=%fused_computation.97 | convolution fusion | flops 3221225472 | bytes 9961472 | tf_op jit(solution)/shard_map/dot_general | solution.py:26
  90.3 0.0 copy-start.5
  90.3 6.9 %fusion.15 = f32[1024,128]{1,0:T(8,128)S(1)} fusion(f32[1024,2048]{1,0:T(8,128)S(1)} %bitcast.63, f32[2048,128]{1,0:T(8,128)S(1)} %bitcast.89), kind=kOutput, calls=%fused_computation.98 | convolution fusion | flops 3221225472 | bytes 9961472 | tf_op jit(solution)/shard_map/dot_general | solution.py:26
  97.2 0.0 slice-start.17
  97.2 6.7 %fusion.16 = f32[1024,128]{1,0:T(8,128)S(1)} fusion(f32[1024,2048]{1,0:T(8,128)S(1)} %get-tuple-element.11, f32[2048,128]{1,0:T(8,128)S(1)} %bitcast.88), kind=kOutput, calls=%fused_computation.99 | convolution fusion | flops 3221225472 | bytes 9961472 | tf_op jit(solution)/shard_map/dot_general | solution.py:26
  104.0 8.5 %fusion.5 = f32[1024,128]{1,0:T(8,128)} fusion(f32[1024,128]{1,0:T(8,128)S(1)} %fusion.16, f32[1024,128]{1,0:T(8,128)S(1)} %fusion.15, f32[1024,128]{1,0:T(8,128)S(1)} %fusion.14, f32[1024,128]{1,0:T(8,128)S(1)} %fusion.13, f32[1024,128]{1,0:T(8,128)S(1)} %fusion.12, f32[1024,128]{1,0:T(8,128)S(1)} %fusion.11, f32[1024,128]{1,0:T(8,128)S(1)} %fusion.10, ...), kind=kOutput, calls=%fused_computation.7 | convolution fusion | flops 3222142976 | bytes 13631488 | tf_op jit(solution)/shard_map/dot_general | solution.py:26
  112.5 0.0 reduce-scatter.3.cloned.1.call-update
  112.5 0.0 all-reduce.2.cloned.1.call-start
  112.5 25.6 %reduce-scatter.3.cloned.1.call-done = f32[256,128]{1,0:T(8,128)} async-done(((f32[1024,128]{1,0:T(8,128)}), f32[256,128]{1,0:T(8,128)}) %reduce-scatter.3.cloned.1.call-update) | async-done | bytes 131088 | tf_op jit(solution)/shard_map/reduce_scatter | solution.py:40
  138.1 2.0 fusion.17
  140.1 0.0 all-reduce.2.cloned.1.call-update
  140.2 0.0 reduce-scatter.5.cloned.1.call-start
  140.2 123.5 %all-reduce.2.cloned.1.call-done = f32[128,128]{0,1:T(8,128)} async-done(((f32[128,128]{0,1:T(8,128)}), f32[128,128]{0,1:T(8,128)}) %all-reduce.2.cloned.1.call-update) | async-done | bytes 65552 | tf_op jit(solution)/shard_map/psum | solution.py:42
  263.7 0.9 copy.5
  264.6 0.9 fusion.8
  265.5 11.7 %cholesky.16 = f32[128,128]{1,0:T(8,128)S(1)} custom-call(f32[128,128]{1,0:T(8,128)S(1)} %fusion.8), custom_call_target="Cholesky" | custom-call | tf_op jit(solution)/shard_map/jit(cholesky)/cholesky | solution.py:42
  277.2 0.6 compare_reduce_fusion
  277.9 0.7 fusion.6
  278.5 9.8 %custom-call.6 = f32[1,128,128]{1,2,0:T(8,128)S(1)} custom-call(f32[1,128,128]{2,1,0:T(8,128)S(1)} %fusion.6), custom_call_target="InvertDiagBlocksLowerTriangular" | custom-call | tf_op jit(solution)/shard_map/triangular_solve | solution.py:45
  288.4 1.2 convolution_multiply_fusion
  289.5 8.8 %all_gather.3 = f32[1024,128]{1,0:T(8,128)S(1)} all-gather(f32[256,128]{1,0:T(8,128)S(1)} %convolution_multiply_fusion), channel_id=1, replica_groups=mesh['tm'=8,'chan'=4] {'chan'}, dimensions={0}, use_global_device_ids=true | all-gather | bytes 655360 | tf_op jit(solution)/shard_map/all_gather | solution.py:48
  298.3 15.9 %fusion.25 = f32[2048,128]{1,0:T(8,128)S(1)} fusion(f32[1024,2048]{1,0:T(8,128)} %copy-done.1, f32[1024,128]{1,0:T(8,128)S(1)} %all_gather.3), kind=kOutput, calls=%fused_computation.108 | convolution fusion | flops 3221225472 | bytes 9961472 | tf_op jit(solution)/shard_map/dot_general | solution.py:58
  314.2 0.0 slice-start.9
  314.2 14.2 %fusion.24 = f32[2048,128]{1,0:T(8,128)S(1)} fusion(f32[1024,2048]{1,0:T(8,128)S(1)} %bitcast.65, f32[1024,128]{1,0:T(8,128)S(1)} %all_gather.3), kind=kOutput, calls=%fused_computation.107 | convolution fusion | flops 3221225472 | bytes 9961472 | tf_op jit(solution)/shard_map/dot_general | solution.py:58
  328.5 14.4 %fusion.23 = f32[2048,128]{1,0:T(8,128)S(1)} fusion(f32[1024,2048]{1,0:T(8,128)S(1)} %bitcast.69, f32[1024,128]{1,0:T(8,128)S(1)} %all_gather.3), kind=kOutput, calls=%fused_computation.106 | convolution fusion | flops 3221225472 | bytes 9961472 | tf_op jit(solution)/shard_map/dot_general | solution.py:58
  343.0 14.2 %fusion.22 = f32[2048,128]{1,0:T(8,128)S(1)} fusion(f32[1024,2048]{1,0:T(8,128)S(1)} %bitcast.71, f32[1024,128]{1,0:T(8,128)S(1)} %all_gather.3), kind=kOutput, calls=%fused_computation.105 | convolution fusion | flops 3221225472 | bytes 9961472 | tf_op jit(solution)/shard_map/dot_general | solution.py:58
  357.2 14.2 %fusion.21 = f32[2048,128]{1,0:T(8,128)S(1)} fusion(f32[1024,2048]{1,0:T(8,128)S(1)} %bitcast.73, f32[1024,128]{1,0:T(8,128)S(1)} %all_gather.3), kind=kOutput, calls=%fused_computation.104 | convolution fusion | flops 3221225472 | bytes 9961472 | tf_op jit(solution)/shard_map/dot_general | solution.py:58
  371.5 14.4 %fusion.20 = f32[2048,128]{1,0:T(8,128)S(1)} fusion(f32[1024,2048]{1,0:T(8,128)S(1)} %bitcast.75, f32[1024,128]{1,0:T(8,128)S(1)} %all_gather.3), kind=kOutput, calls=%fused_computation.103 | convolution fusion | flops 3221225472 | bytes 9961472 | tf_op jit(solution)/shard_map/dot_general | solution.py:58
  386.0 13.9 %fusion.19 = f32[2048,128]{1,0:T(8,128)S(1)} fusion(f32[1024,2048]{1,0:T(8,128)S(1)} %bitcast.61, f32[1024,128]{1,0:T(8,128)S(1)} %all_gather.3), kind=kOutput, calls=%fused_computation.102 | convolution fusion | flops 3221225472 | bytes 9961472 | tf_op jit(solution)/shard_map/dot_general | solution.py:58
  399.9 14.0 %fusion.18 = f32[2048,128]{1,0:T(8,128)S(1)} fusion(f32[1024,2048]{1,0:T(8,128)S(1)} %bitcast.79, f32[1024,128]{1,0:T(8,128)S(1)} %all_gather.3), kind=kOutput, calls=%fused_computation.101 | convolution fusion | flops 3221225472 | bytes 9961472 | tf_op jit(solution)/shard_map/dot_general | solution.py:58
  413.9 0.1 constant_dynamic-update-slice_fusion.10
  414.0 0.1 constant_dynamic-update-slice_fusion.9
  414.0 0.1 constant_dynamic-update-slice_fusion.8
  414.1 0.1 constant_dynamic-update-slice_fusion.7
  414.2 0.1 constant_dynamic-update-slice_fusion.6
  414.3 0.1 constant_dynamic-update-slice_fusion.5
  414.3 0.1 constant_dynamic-update-slice_fusion.4
  414.4 0.1 constant_dynamic-update-slice_fusion.3
  414.5 4.1 broadcast_multiply_fusion
  418.6 0.0 reduce-scatter.5.cloned.1.call-update
  418.6 146.5 %reduce-scatter.5.cloned.1.call-done = f32[8,256,128]{2,1,0:T(8,128)} async-done(((f32[64,256,128]{2,1,0:T(8,128)}), f32[8,256,128]{2,1,0:T(8,128)}) %reduce-scatter.5.cloned.1.call-update) | async-done | bytes 1048592 | tf_op jit(solution)/shard_map/reduce_scatter | solution.py:62
  565.2 0.8 copy.73
  (59 shorter events, 0.1 us)
Async XLA Ops:
  7.2 131.0 %reduce-scatter.3.cloned.1.call-start = ((), (), s32[]{:S(2)}) async-start(), calls=%async_computation.2 | async-start | bytes 655360 | tf_op jit(solution)/shard_map/reduce_scatter | solution.py:40
  8.1 7.3 %copy-start.6 = (f32[1024,256]{1,0:T(8,128)S(1)}, f32[1024,256]{1,0:T(8,128)}, u32[]{:S(2)}) copy-start(f32[1024,256]{1,0:T(8,128)} %param.2) | copy-start | bytes 3145732
  8.1 8.4 %collective-permute-start = (f32[63,256]{1,0:T(8,128)S(1)}, f32[63,256]{1,0:T(8,128)S(1)}, u32[]{:S(2)}, u32[]{:S(2)}) collective-permute-start(f32[63,256]{1,0:T(8,128)S(1)} %slice.226), channel_id=1, source_target_pairs={{4,0},{8,4},{12,8},{16,12},{20,16},{24,20},{28,24},{5,1},{9,5},{13... | collective-permute-start | bytes 193544 | tf_op jit(solution)/shard_map/ppermute | solution.py:13
  38.6 28.6 %copy-start = (f32[1024,2048]{1,0:T(8,128)}, f32[1024,2048]{1,0:T(8,128)S(1)}, u32[]{:S(2)}) copy-start(f32[1024,2048]{1,0:T(8,128)S(1)} %get-tuple-element.17) | copy-start | bytes 25165828
  38.6 58.6 %copy-start.1 = (f32[1024,2048]{1,0:T(8,128)}, f32[1024,2048]{1,0:T(8,128)S(1)}, u32[]{:S(2)}) copy-start(f32[1024,2048]{1,0:T(8,128)S(1)} %get-tuple-element.11) | copy-start | bytes 25165828
  38.6 19.3 %copy-start.4 = (f32[8,256,128]{2,1,0:T(8,128)S(1)}, f32[8,256,128]{2,1,0:T(8,128)}, u32[]{:S(2)}) copy-start(f32[8,256,128]{2,1,0:T(8,128)} %get-tuple-element.6) | copy-start | bytes 3145732
  38.6 28.6 %copy-start.3 = (f32[8,256,128]{2,1,0:T(8,128)S(1)}, f32[8,256,128]{2,1,0:T(8,128)}, u32[]{:S(2)}) copy-start(f32[8,256,128]{2,1,0:T(8,128)} %get-tuple-element.5) | copy-start | bytes 3145732
  57.9 9.3 %copy-start.2 = (f32[1024,2048]{1,0:T(8,128)S(1)}, f32[1024,2048]{1,0:T(8,128)}, u32[]{:S(2)}) copy-start(f32[1024,2048]{1,0:T(8,128)} %get-tuple-element.15) | copy-start | bytes 25165828
  58.0 25.6 %slice-start.6 = ((s8[8388608]{0:T(1024)(128)(4,1)}), s8[4194304]{0:T(1024)(128)(4,1)S(1)}, s32[]{:S(2)}) async-start(s8[8388608]{0:T(1024)(128)(4,1)} %bitcast.66), calls=%async_computation.11 | async-start | bytes 8388608
  67.2 16.4 %slice-start.7 = ((s8[8388608]{0:T(1024)(128)(4,1)}), s8[4194304]{0:T(1024)(128)(4,1)S(1)}, s32[]{:S(2)}) async-start(s8[8388608]{0:T(1024)(128)(4,1)} %bitcast.66), calls=%async_computation.12 | async-start | bytes 8388608
  73.9 16.4 %slice-start.2 = ((s8[8388608]{0:T(1024)(128)(4,1)}), s8[4194304]{0:T(1024)(128)(4,1)S(1)}, s32[]{:S(2)}) async-start(s8[8388608]{0:T(1024)(128)(4,1)} %bitcast.62), calls=%async_computation.7 | async-start | bytes 8388608
  83.6 6.7 %slice-start.3 = ((s8[8388608]{0:T(1024)(128)(4,1)}), s8[4194304]{0:T(1024)(128)(4,1)S(1)}, s32[]{:S(2)}) async-start(s8[8388608]{0:T(1024)(128)(4,1)} %bitcast.62), calls=%async_computation.8 | async-start | bytes 8388608
  90.3 13.6 %slice-start.16 = ((s8[8388608]{0:T(1024)(128)(4,1)}), s8[4194304]{0:T(1024)(128)(4,1)S(1)}, s32[]{:S(2)}) async-start(s8[8388608]{0:T(1024)(128)(4,1)} %bitcast.76), calls=%async_computation.21 | async-start | bytes 8388608
  90.3 13.6 %copy-start.5 = (f32[8,256,128]{2,1,0:T(8,128)S(1)}, f32[8,256,128]{2,1,0:T(8,128)}, u32[]{:S(2)}) copy-start(f32[8,256,128]{2,1,0:T(8,128)} %get-tuple-element.2) | copy-start | bytes 3145732
  97.2 6.7 %slice-start.17 = ((s8[8388608]{0:T(1024)(128)(4,1)}), s8[4194304]{0:T(1024)(128)(4,1)S(1)}, s32[]{:S(2)}) async-start(s8[8388608]{0:T(1024)(128)(4,1)} %bitcast.76), calls=%async_computation.22 | async-start | bytes 8388608
  112.5 151.2 %all-reduce.2.cloned.1.call-start = ((), (), s32[]{:S(2)}) async-start(), calls=%async_computation.3 | async-start | bytes 131072 | tf_op jit(solution)/shard_map/psum | solution.py:42
  140.2 425.0 %reduce-scatter.5.cloned.1.call-start = ((), (), s32[]{:S(2)}) async-start(), calls=%async_computation.4 | async-start | bytes 9437184 | tf_op jit(solution)/shard_map/reduce_scatter | solution.py:62
  289.5 24.7 %slice-start.4 = ((s8[8388608]{0:T(1024)(128)(4,1)}), s8[4194304]{0:T(1024)(128)(4,1)S(1)}, s32[]{:S(2)}) async-start(s8[8388608]{0:T(1024)(128)(4,1)} %bitcast.64), calls=%async_computation.9 | async-start | bytes 8388608
  298.3 15.9 %slice-start.5 = ((s8[8388608]{0:T(1024)(128)(4,1)}), s8[4194304]{0:T(1024)(128)(4,1)S(1)}, s32[]{:S(2)}) async-start(s8[8388608]{0:T(1024)(128)(4,1)} %bitcast.64), calls=%async_computation.10 | async-start | bytes 8388608
  298.3 30.2 %slice-start.8 = ((s8[8388608]{0:T(1024)(128)(4,1)}), s8[4194304]{0:T(1024)(128)(4,1)S(1)}, s32[]{:S(2)}) async-start(s8[8388608]{0:T(1024)(128)(4,1)} %bitcast.68), calls=%async_computation.13 | async-start | bytes 8388608
  314.2 14.3 %slice-start.9 = ((s8[8388608]{0:T(1024)(128)(4,1)}), s8[4194304]{0:T(1024)(128)(4,1)S(1)}, s32[]{:S(2)}) async-start(s8[8388608]{0:T(1024)(128)(4,1)} %bitcast.68), calls=%async_computation.14 | async-start | bytes 8388608
  314.2 28.7 %slice-start.10 = ((s8[8388608]{0:T(1024)(128)(4,1)}), s8[4194304]{0:T(1024)(128)(4,1)S(1)}, s32[]{:S(2)}) async-start(s8[8388608]{0:T(1024)(128)(4,1)} %bitcast.70), calls=%async_computation.15 | async-start | bytes 8388608
  328.5 14.5 %slice-start.11 = ((s8[8388608]{0:T(1024)(128)(4,1)}), s8[4194304]{0:T(1024)(128)(4,1)S(1)}, s32[]{:S(2)}) async-start(s8[8388608]{0:T(1024)(128)(4,1)} %bitcast.70), calls=%async_computation.16 | async-start | bytes 8388608
  328.5 28.7 %slice-start.12 = ((s8[8388608]{0:T(1024)(128)(4,1)}), s8[4194304]{0:T(1024)(128)(4,1)S(1)}, s32[]{:S(2)}) async-start(s8[8388608]{0:T(1024)(128)(4,1)} %bitcast.72), calls=%async_computation.17 | async-start | bytes 8388608
  343.0 14.2 %slice-start.13 = ((s8[8388608]{0:T(1024)(128)(4,1)}), s8[4194304]{0:T(1024)(128)(4,1)S(1)}, s32[]{:S(2)}) async-start(s8[8388608]{0:T(1024)(128)(4,1)} %bitcast.72), calls=%async_computation.18 | async-start | bytes 8388608
  343.0 28.5 %slice-start.14 = ((s8[8388608]{0:T(1024)(128)(4,1)}), s8[4194304]{0:T(1024)(128)(4,1)S(1)}, s32[]{:S(2)}) async-start(s8[8388608]{0:T(1024)(128)(4,1)} %bitcast.74), calls=%async_computation.19 | async-start | bytes 8388608
  357.2 14.3 %slice-start.15 = ((s8[8388608]{0:T(1024)(128)(4,1)}), s8[4194304]{0:T(1024)(128)(4,1)S(1)}, s32[]{:S(2)}) async-start(s8[8388608]{0:T(1024)(128)(4,1)} %bitcast.74), calls=%async_computation.20 | async-start | bytes 8388608
  357.2 28.7 %slice-start = ((s8[8388608]{0:T(1024)(128)(4,1)}), s8[4194304]{0:T(1024)(128)(4,1)S(1)}, s32[]{:S(2)}) async-start(s8[8388608]{0:T(1024)(128)(4,1)} %bitcast.60), calls=%async_computation.5 | async-start | bytes 8388608
  371.5 14.5 %slice-start.1 = ((s8[8388608]{0:T(1024)(128)(4,1)}), s8[4194304]{0:T(1024)(128)(4,1)S(1)}, s32[]{:S(2)}) async-start(s8[8388608]{0:T(1024)(128)(4,1)} %bitcast.60), calls=%async_computation.6 | async-start | bytes 8388608
  371.5 28.4 %slice-start.18 = ((s8[8388608]{0:T(1024)(128)(4,1)}), s8[4194304]{0:T(1024)(128)(4,1)S(1)}, s32[]{:S(2)}) async-start(s8[8388608]{0:T(1024)(128)(4,1)} %bitcast.78), calls=%async_computation.23 | async-start | bytes 8388608
  385.9 13.9 %slice-start.19 = ((s8[8388608]{0:T(1024)(128)(4,1)}), s8[4194304]{0:T(1024)(128)(4,1)S(1)}, s32[]{:S(2)}) async-start(s8[8388608]{0:T(1024)(128)(4,1)} %bitcast.78), calls=%async_computation.24 | async-start | bytes 8388608
Sparse Core Ops, SparseCore 0:
  112.6 25.5 reduce-scatter.2
  144.3 119.3 all-reduce.1
  418.8 146.3 reduce-scatter.4
where the time goes:
time: 582 us; the launch traced here: 573 us
  waiting for transfers between devices  296 us (51%)
  matrix products  192 us (33%)
  local copies, waits for them, and re-layouts  32.4 us (6%)
  other arithmetic  27.8 us (5%)
  between operations  14.6 us (3%)
  blocking collectives  8.78 us (2%)
    reduce_scatter x1, waiting for transfers between devices, on_device(): lax.psum_scatter(jnp.concatenate(pieces, axis=0) * scale, 'tm', scatter_d...  147 us
    psum x1, waiting for transfers between devices, on_device(): lower = jnp.linalg.cholesky(lax.psum(gram, ('tm', 'chan')))  123 us
    dot_general x8, matrix products, on_device(): lax.dot_general(block, basis, (((0,), (0,)), ((), ())), precision=hi, pre...  115 us
    dot_general x8, matrix products, sketch_part(): jnp.dot(block, weights, precision=hi, preferred_element_type=jnp.float32)  73.6 us
    reduce_scatter x1, waiting for transfers between devices, on_device(): lax.psum_scatter(partial_value, 'chan', scatter_dimension=0, tiled=True)  25.6 us
    unnamed x70, local copies, waits for them, and re-layouts  21.8 us
    another operation x3, other arithmetic, on_device(): lower = jnp.linalg.cholesky(lax.psum(gram, ('tm', 'chan')))  12.4 us
  transfers between devices with their start and end apart: 4, of which 3 were waited for; matrix products, arithmetic and copies ran while one was open for 1% of the time, Pallas kernels for 0%

commit v1 on v0

--- a/solution.py
+++ b/solution.py
@@ -39,7 +39,7 @@
     partial_value = sketch_part(extended, test_matrix, rows)
     own = lax.psum_scatter(partial_value, "chan", scatter_dimension=0, tiled=True)
     gram = jnp.dot(own.T, own, precision=hi, preferred_element_type=jnp.float32)
-    lower = jnp.linalg.cholesky(lax.psum(gram, ("tm", "chan")))
+    lower = jnp.linalg.cholesky(lax.psum(lax.psum(gram, "tm"), "chan"))
     root = jnp.sqrt(jnp.float32(total_rows))
     share = (
         lax.linalg.triangular_solve(lower, own, left_side=False, lower=True, transpose_a=True)

time: 582 us -> 562 us (0.966)
  waiting for transfers between devices: 296 us -> 279 us
    psum x1 -> x2, waiting for transfers between devices: 123 us -> 105 us  [on_device(): lower = jnp.linalg.cholesky(lax.psum(lax.psum(gram, 'tm'), 'chan'))]
    unnamed x70 -> x74, local copies, waits for them, and re-layouts: 21.8 us -> 21.9 us
  transfers between devices with their start and end apart: 4 -> 5, of which waited for: 3 -> 4; matrix products, arithmetic and copies ran while one was open for 1% -> 1% of each run, Pallas kernels for 0% -> 0%
where the time goes in v1:
time: 562 us; the launch traced here: 553 us
  waiting for transfers between devices  279 us (50%)
  matrix products  191 us (34%)
  local copies, waits for them, and re-layouts  32.3 us (6%)
  other arithmetic  27.8 us (5%)
  between operations  14.7 us (3%)
  blocking collectives  7.1 us (1%)
    reduce_scatter x1, waiting for transfers between devices, on_device(): lax.psum_scatter(jnp.concatenate(pieces, axis=0) * scale, 'tm', scatter_d...  148 us
    dot_general x8, matrix products, on_device(): lax.dot_general(block, basis, (((0,), (0,)), ((), ())), precision=hi, pre...  115 us
    psum x2, waiting for transfers between devices, on_device(): lower = jnp.linalg.cholesky(lax.psum(lax.psum(gram, 'tm'), 'chan'))  105 us
    dot_general x8, matrix products, sketch_part(): jnp.dot(block, weights, precision=hi, preferred_element_type=jnp.float32)  72.2 us
    reduce_scatter x1, waiting for transfers between devices, on_device(): lax.psum_scatter(partial_value, 'chan', scatter_dimension=0, tiled=True)  25.6 us
    unnamed x74, local copies, waits for them, and re-layouts  21.9 us
    another operation x3, other arithmetic, on_device(): lower = jnp.linalg.cholesky(lax.psum(lax.psum(gram, 'tm'), 'chan'))  12.4 us
  transfers between devices with their start and end apart: 5, of which 4 were waited for; matrix products, arithmetic and copies ran while one was open for 1% of the time, Pallas kernels for 0%

profile of v1, /device:TPU:0, one launch (start us, length us, event | category | flops | bytes accessed | tf_op | source)
XLA Modules:
  0.0 553.0 jit_solution(3461954694918278827)
XLA Ops:
  7.2 0.0 reduce-scatter.3.cloned.1.call-start
  7.2 0.8 slice.226
  8.1 1.4 collective-permute-start
  9.5 5.8 %fusion.9 = (f32[8,256,128]{2,1,0:T(8,128)}, f32[8,256,128]{2,1,0:T(8,128)S(1)}, f32[8,256,128]{2,1,0:T(8,128)S(1)}, f32[8,256,128]{2,1,0:T(8,128)}, f32[8,256,1...) fusion(f32[64,256,128]{2,1,0:T(8,128)} %param.3), kind=kLoop, calls=%fused_computation.92 | loop fusion | bytes 16777216 | tf_op jit(solution)/shard_map/slice | solution.py:25
  15.3 1.2 constant_dynamic-update-slice_fusion.2
  16.5 0.0 collective-permute-done
  16.5 2.4 slice_dynamic-update-slice_fusion.55
  18.9 2.8 slice_dynamic-update-slice_fusion.62
  21.7 2.9 slice_dynamic-update-slice_fusion.61
  24.6 2.9 slice_dynamic-update-slice_fusion.60
  27.5 2.8 slice_dynamic-update-slice_fusion.59
  30.3 2.9 slice_dynamic-update-slice_fusion.58
  33.2 2.7 slice_dynamic-update-slice_fusion.57
  35.8 2.7 slice_dynamic-update-slice_fusion.56
  38.6 20.2 %fusion.10 = f32[1024,128]{1,0:T(8,128)S(1)} fusion(f32[1024,2048]{1,0:T(8,128)S(1)} %get-tuple-element.17, f32[2048,128]{1,0:T(8,128)} %bitcast.94), kind=kOutput, calls=%fused_computation.93 | convolution fusion | flops 3221225472 | bytes 9961472 | tf_op jit(solution)/shard_map/dot_general | solution.py:26
  58.8 9.2 %fusion.11 = f32[1024,128]{1,0:T(8,128)S(1)} fusion(f32[1024,2048]{1,0:T(8,128)} %get-tuple-element.16, f32[2048,128]{1,0:T(8,128)S(1)} %bitcast.93), kind=kOutput, calls=%fused_computation.94 | convolution fusion | flops 3221225472 | bytes 9961472 | tf_op jit(solution)/shard_map/dot_general | solution.py:26
  68.1 0.0 slice-start.7
  68.1 7.5 %fusion.12 = f32[1024,128]{1,0:T(8,128)} fusion(f32[1024,2048]{1,0:T(8,128)S(1)} %copy-done.3, f32[2048,128]{1,0:T(8,128)S(1)} %bitcast.92), kind=kOutput, calls=%fused_computation.95 | convolution fusion | flops 3221225472 | bytes 9961472 | tf_op jit(solution)/shard_map/dot_general | solution.py:26
  75.6 7.1 %fusion.13 = f32[1024,128]{1,0:T(8,128)S(1)} fusion(f32[1024,2048]{1,0:T(8,128)S(1)} %copy-done.2, f32[2048,128]{1,0:T(8,128)S(1)} %bitcast.91), kind=kOutput, calls=%fused_computation.96 | convolution fusion | flops 3221225472 | bytes 9961472 | tf_op jit(solution)/shard_map/dot_general | solution.py:26
  82.7 6.7 %fusion.14 = f32[1024,128]{1,0:T(8,128)S(1)} fusion(f32[1024,2048]{1,0:T(8,128)S(1)} %bitcast.67, f32[2048,128]{1,0:T(8,128)S(1)} %bitcast.90), kind=kOutput, calls=%fused_computation.97 | convolution fusion | flops 3221225472 | bytes 9961472 | tf_op jit(solution)/shard_map/dot_general | solution.py:26
  89.4 0.0 slice-start.16
  89.4 0.0 copy-start.6
  89.4 0.0 copy-start.7
  89.4 6.9 %fusion.15 = f32[1024,128]{1,0:T(8,128)S(1)} fusion(f32[1024,2048]{1,0:T(8,128)S(1)} %bitcast.63, f32[2048,128]{1,0:T(8,128)S(1)} %bitcast.89), kind=kOutput, calls=%fused_computation.98 | convolution fusion | flops 3221225472 | bytes 9961472 | tf_op jit(solution)/shard_map/dot_general | solution.py:26
  96.3 6.7 %fusion.16 = f32[1024,128]{1,0:T(8,128)S(1)} fusion(f32[1024,2048]{1,0:T(8,128)S(1)} %get-tuple-element.11, f32[2048,128]{1,0:T(8,128)S(1)} %bitcast.88), kind=kOutput, calls=%fused_computation.99 | convolution fusion | flops 3221225472 | bytes 9961472 | tf_op jit(solution)/shard_map/dot_general | solution.py:26
  103.1 8.0 %fusion.5 = f32[1024,128]{1,0:T(8,128)} fusion(f32[1024,128]{1,0:T(8,128)S(1)} %fusion.16, f32[1024,128]{1,0:T(8,128)S(1)} %fusion.15, f32[1024,128]{1,0:T(8,128)S(1)} %fusion.14, f32[1024,128]{1,0:T(8,128)S(1)} %fusion.13, f32[1024,128]{1,0:T(8,128)S(1)} %copy-done.7, f32[1024,128]{1,0:T(8,128)S(1)} %fusion.11, f32[1024,128]{1,0:T(8,128)S(1)} %fusion.10, ...), kind=kOutput, calls=%fused_computation.7 | convolution fusion | flops 3222142976 | bytes 13631488 | tf_op jit(solution)/shard_map/dot_general | solution.py:26
  111.1 0.0 reduce-scatter.3.cloned.1.call-update
  111.1 0.0 all-reduce.3.cloned.1.call-start
  111.2 25.6 %reduce-scatter.3.cloned.1.call-done = f32[256,128]{1,0:T(8,128)} async-done(((f32[1024,128]{1,0:T(8,128)}), f32[256,128]{1,0:T(8,128)}) %reduce-scatter.3.cloned.1.call-update) | async-done | bytes 131088 | tf_op jit(solution)/shard_map/reduce_scatter | solution.py:40
  136.8 2.0 fusion.17
  138.8 0.0 all-reduce.3.cloned.1.call-update
  138.8 0.0 all-reduce.5.cloned.1.call-start
  138.9 71.2 %all-reduce.3.cloned.1.call-done = f32[128,128]{0,1:T(8,128)} async-done(((f32[128,128]{0,1:T(8,128)}), f32[128,128]{0,1:T(8,128)}) %all-reduce.3.cloned.1.call-update) | async-done | bytes 65552 | tf_op jit(solution)/shard_map/psum | solution.py:42
  210.1 0.0 all-reduce.5.cloned.1.call-update
  210.1 0.3 reduce-scatter.5.cloned.1.call-start
  210.4 33.5 %all-reduce.5.cloned.1.call-done = f32[128,128]{0,1:T(8,128)} async-done(((f32[128,128]{0,1:T(8,128)}), f32[128,128]{0,1:T(8,128)}) %all-reduce.5.cloned.1.call-update) | async-done | bytes 65552 | tf_op jit(solution)/shard_map/psum | solution.py:42
  243.9 0.9 copy.5
  244.8 0.9 fusion.8
  245.7 11.7 %cholesky.16 = f32[128,128]{1,0:T(8,128)S(1)} custom-call(f32[128,128]{1,0:T(8,128)S(1)} %fusion.8), custom_call_target="Cholesky" | custom-call | tf_op jit(solution)/shard_map/jit(cholesky)/cholesky | solution.py:42
  257.4 0.6 compare_reduce_fusion
  258.1 0.7 fusion.6
  258.7 9.8 %custom-call.6 = f32[1,128,128]{1,2,0:T(8,128)S(1)} custom-call(f32[1,128,128]{2,1,0:T(8,128)S(1)} %fusion.6), custom_call_target="InvertDiagBlocksLowerTriangular" | custom-call | tf_op jit(solution)/shard_map/triangular_solve | solution.py:45
  268.5 1.2 convolution_multiply_fusion
  269.7 7.1 %all_gather.3 = f32[1024,128]{1,0:T(8,128)S(1)} all-gather(f32[256,128]{1,0:T(8,128)S(1)} %convolution_multiply_fusion), channel_id=1, replica_groups=mesh['tm'=8,'chan'=4] {'chan'}, dimensions={0}, use_global_device_ids=true | all-gather | bytes 655360 | tf_op jit(solution)/shard_map/all_gather | solution.py:48
  276.8 15.9 %fusion.25 = f32[2048,128]{1,0:T(8,128)S(1)} fusion(f32[1024,2048]{1,0:T(8,128)} %copy-done.1, f32[1024,128]{1,0:T(8,128)S(1)} %all_gather.3), kind=kOutput, calls=%fused_computation.108 | convolution fusion | flops 3221225472 | bytes 9961472 | tf_op jit(solution)/shard_map/dot_general | solution.py:58
  292.8 14.2 %fusion.24 = f32[2048,128]{1,0:T(8,128)S(1)} fusion(f32[1024,2048]{1,0:T(8,128)S(1)} %bitcast.65, f32[1024,128]{1,0:T(8,128)S(1)} %all_gather.3), kind=kOutput, calls=%fused_computation.107 | convolution fusion | flops 3221225472 | bytes 9961472 | tf_op jit(solution)/shard_map/dot_general | solution.py:58
  307.0 14.4 %fusion.23 = f32[2048,128]{1,0:T(8,128)S(1)} fusion(f32[1024,2048]{1,0:T(8,128)S(1)} %bitcast.69, f32[1024,128]{1,0:T(8,128)S(1)} %all_gather.3), kind=kOutput, calls=%fused_computation.106 | convolution fusion | flops 3221225472 | bytes 9961472 | tf_op jit(solution)/shard_map/dot_general | solution.py:58
  321.5 14.2 %fusion.22 = f32[2048,128]{1,0:T(8,128)S(1)} fusion(f32[1024,2048]{1,0:T(8,128)S(1)} %bitcast.71, f32[1024,128]{1,0:T(8,128)S(1)} %all_gather.3), kind=kOutput, calls=%fused_computation.105 | convolution fusion | flops 3221225472 | bytes 9961472 | tf_op jit(solution)/shard_map/dot_general | solution.py:58
  335.7 14.2 %fusion.21 = f32[2048,128]{1,0:T(8,128)S(1)} fusion(f32[1024,2048]{1,0:T(8,128)S(1)} %bitcast.73, f32[1024,128]{1,0:T(8,128)S(1)} %all_gather.3), kind=kOutput, calls=%fused_computation.104 | convolution fusion | flops 3221225472 | bytes 9961472 | tf_op jit(solution)/shard_map/dot_general | solution.py:58
  350.0 14.4 %fusion.20 = f32[2048,128]{1,0:T(8,128)S(1)} fusion(f32[1024,2048]{1,0:T(8,128)S(1)} %bitcast.75, f32[1024,128]{1,0:T(8,128)S(1)} %all_gather.3), kind=kOutput, calls=%fused_computation.103 | convolution fusion | flops 3221225472 | bytes 9961472 | tf_op jit(solution)/shard_map/dot_general | solution.py:58
  364.5 13.9 %fusion.19 = f32[2048,128]{1,0:T(8,128)S(1)} fusion(f32[1024,2048]{1,0:T(8,128)S(1)} %bitcast.61, f32[1024,128]{1,0:T(8,128)S(1)} %all_gather.3), kind=kOutput, calls=%fused_computation.102 | convolution fusion | flops 3221225472 | bytes 9961472 | tf_op jit(solution)/shard_map/dot_general | solution.py:58
  378.4 14.0 %fusion.18 = f32[2048,128]{1,0:T(8,128)S(1)} fusion(f32[1024,2048]{1,0:T(8,128)S(1)} %bitcast.79, f32[1024,128]{1,0:T(8,128)S(1)} %all_gather.3), kind=kOutput, calls=%fused_computation.101 | convolution fusion | flops 3221225472 | bytes 9961472 | tf_op jit(solution)/shard_map/dot_general | solution.py:58
  392.4 0.1 constant_dynamic-update-slice_fusion.10
  392.5 0.1 constant_dynamic-update-slice_fusion.9
  392.5 0.1 constant_dynamic-update-slice_fusion.8
  392.6 0.1 constant_dynamic-update-slice_fusion.7
  392.7 0.1 constant_dynamic-update-slice_fusion.6
  392.8 0.1 constant_dynamic-update-slice_fusion.5
  392.9 0.1 constant_dynamic-update-slice_fusion.4
  392.9 0.1 constant_dynamic-update-slice_fusion.3
  393.0 4.1 broadcast_multiply_fusion
  397.1 0.0 reduce-scatter.5.cloned.1.call-update
  397.2 148.3 %reduce-scatter.5.cloned.1.call-done = f32[8,256,128]{2,1,0:T(8,128)} async-done(((f32[64,256,128]{2,1,0:T(8,128)}), f32[8,256,128]{2,1,0:T(8,128)}) %reduce-scatter.5.cloned.1.call-update) | async-done | bytes 1048592 | tf_op jit(solution)/shard_map/reduce_scatter | solution.py:62
  545.4 0.8 copy.74
  (66 shorter events, 0.2 us)
Async XLA Ops:
  7.2 129.6 %reduce-scatter.3.cloned.1.call-start = ((), (), s32[]{:S(2)}) async-start(), calls=%async_computation.2 | async-start | bytes 655360 | tf_op jit(solution)/shard_map/reduce_scatter | solution.py:40
  8.1 7.2 %copy-start.8 = (f32[1024,256]{1,0:T(8,128)S(1)}, f32[1024,256]{1,0:T(8,128)}, u32[]{:S(2)}) copy-start(f32[1024,256]{1,0:T(8,128)} %param.2) | copy-start | bytes 3145732
  8.1 8.4 %collective-permute-start = (f32[63,256]{1,0:T(8,128)S(1)}, f32[63,256]{1,0:T(8,128)S(1)}, u32[]{:S(2)}, u32[]{:S(2)}) collective-permute-start(f32[63,256]{1,0:T(8,128)S(1)} %slice.226), channel_id=1, source_target_pairs={{4,0},{8,4},{12,8},{16,12},{20,16},{24,20},{28,24},{5,1},{9,5},{13... | collective-permute-start | bytes 193544 | tf_op jit(solution)/shard_map/ppermute | solution.py:13
  38.6 29.5 %copy-start = (f32[1024,2048]{1,0:T(8,128)}, f32[1024,2048]{1,0:T(8,128)S(1)}, u32[]{:S(2)}) copy-start(f32[1024,2048]{1,0:T(8,128)S(1)} %get-tuple-element.17) | copy-start | bytes 25165828
  38.6 57.8 %copy-start.1 = (f32[1024,2048]{1,0:T(8,128)}, f32[1024,2048]{1,0:T(8,128)S(1)}, u32[]{:S(2)}) copy-start(f32[1024,2048]{1,0:T(8,128)S(1)} %get-tuple-element.11) | copy-start | bytes 25165828
  38.6 20.2 %copy-start.5 = (f32[8,256,128]{2,1,0:T(8,128)S(1)}, f32[8,256,128]{2,1,0:T(8,128)}, u32[]{:S(2)}) copy-start(f32[8,256,128]{2,1,0:T(8,128)} %get-tuple-element.6) | copy-start | bytes 3145732
  38.6 29.5 %copy-start.4 = (f32[8,256,128]{2,1,0:T(8,128)S(1)}, f32[8,256,128]{2,1,0:T(8,128)}, u32[]{:S(2)}) copy-start(f32[8,256,128]{2,1,0:T(8,128)} %get-tuple-element.5) | copy-start | bytes 3145732
  58.8 9.3 %copy-start.3 = (f32[1024,2048]{1,0:T(8,128)S(1)}, f32[1024,2048]{1,0:T(8,128)}, u32[]{:S(2)}) copy-start(f32[1024,2048]{1,0:T(8,128)} %get-tuple-element.15) | copy-start | bytes 25165828
  58.8 23.9 %slice-start.6 = ((s8[8388608]{0:T(1024)(128)(4,1)}), s8[4194304]{0:T(1024)(128)(4,1)S(1)}, s32[]{:S(2)}) async-start(s8[8388608]{0:T(1024)(128)(4,1)} %bitcast.66), calls=%async_computation.12 | async-start | bytes 8388608
  68.1 7.5 %copy-start.2 = (f32[1024,2048]{1,0:T(8,128)S(1)}, f32[1024,2048]{1,0:T(8,128)}, u32[]{:S(2)}) copy-start(f32[1024,2048]{1,0:T(8,128)} %get-tuple-element.14) | copy-start | bytes 25165828
  68.1 14.6 %slice-start.7 = ((s8[8388608]{0:T(1024)(128)(4,1)}), s8[4194304]{0:T(1024)(128)(4,1)S(1)}, s32[]{:S(2)}) async-start(s8[8388608]{0:T(1024)(128)(4,1)} %bitcast.66), calls=%async_computation.13 | async-start | bytes 8388608
  75.6 13.8 %slice-start.2 = ((s8[8388608]{0:T(1024)(128)(4,1)}), s8[4194304]{0:T(1024)(128)(4,1)S(1)}, s32[]{:S(2)}) async-start(s8[8388608]{0:T(1024)(128)(4,1)} %bitcast.62), calls=%async_computation.8 | async-start | bytes 8388608
  82.7 6.7 %slice-start.3 = ((s8[8388608]{0:T(1024)(128)(4,1)}), s8[4194304]{0:T(1024)(128)(4,1)S(1)}, s32[]{:S(2)}) async-start(s8[8388608]{0:T(1024)(128)(4,1)} %bitcast.62), calls=%async_computation.9 | async-start | bytes 8388608
  89.4 13.6 %slice-start.16 = ((s8[8388608]{0:T(1024)(128)(4,1)}), s8[4194304]{0:T(1024)(128)(4,1)S(1)}, s32[]{:S(2)}) async-start(s8[8388608]{0:T(1024)(128)(4,1)} %bitcast.76), calls=%async_computation.22 | async-start | bytes 8388608
  89.4 13.6 %copy-start.6 = (f32[8,256,128]{2,1,0:T(8,128)S(1)}, f32[8,256,128]{2,1,0:T(8,128)}, u32[]{:S(2)}) copy-start(f32[8,256,128]{2,1,0:T(8,128)} %get-tuple-element.2) | copy-start | bytes 3145732
  89.4 13.6 %copy-start.7 = (f32[1024,128]{1,0:T(8,128)S(1)}, f32[1024,128]{1,0:T(8,128)}, u32[]{:S(2)}) copy-start(f32[1024,128]{1,0:T(8,128)} %fusion.12) | copy-start | bytes 1572868
  96.3 6.7 %slice-start.17 = ((s8[8388608]{0:T(1024)(128)(4,1)}), s8[4194304]{0:T(1024)(128)(4,1)S(1)}, s32[]{:S(2)}) async-start(s8[8388608]{0:T(1024)(128)(4,1)} %bitcast.76), calls=%async_computation.23 | async-start | bytes 8388608
  111.1 98.9 %all-reduce.3.cloned.1.call-start = ((), (), s32[]{:S(2)}) async-start(), calls=%async_computation.3 | async-start | bytes 131072 | tf_op jit(solution)/shard_map/psum | solution.py:42
  138.8 105.1 %all-reduce.5.cloned.1.call-start = ((), (), s32[]{:S(2)}) async-start(), calls=%async_computation.4 | async-start | bytes 131072 | tf_op jit(solution)/shard_map/psum | solution.py:42
  210.1 335.3 %reduce-scatter.5.cloned.1.call-start = ((), (), s32[]{:S(2)}) async-start(), calls=%async_computation.5 | async-start | bytes 9437184 | tf_op jit(solution)/shard_map/reduce_scatter | solution.py:62
  269.7 23.0 %slice-start.4 = ((s8[8388608]{0:T(1024)(128)(4,1)}), s8[4194304]{0:T(1024)(128)(4,1)S(1)}, s32[]{:S(2)}) async-start(s8[8388608]{0:T(1024)(128)(4,1)} %bitcast.64), calls=%async_computation.10 | async-start | bytes 8388608
  276.8 15.9 %slice-start.5 = ((s8[8388608]{0:T(1024)(128)(4,1)}), s8[4194304]{0:T(1024)(128)(4,1)S(1)}, s32[]{:S(2)}) async-start(s8[8388608]{0:T(1024)(128)(4,1)} %bitcast.64), calls=%async_computation.11 | async-start | bytes 8388608
  276.8 30.2 %slice-start.8 = ((s8[8388608]{0:T(1024)(128)(4,1)}), s8[4194304]{0:T(1024)(128)(4,1)S(1)}, s32[]{:S(2)}) async-start(s8[8388608]{0:T(1024)(128)(4,1)} %bitcast.68), calls=%async_computation.14 | async-start | bytes 8388608
  292.7 14.3 %slice-start.9 = ((s8[8388608]{0:T(1024)(128)(4,1)}), s8[4194304]{0:T(1024)(128)(4,1)S(1)}, s32[]{:S(2)}) async-start(s8[8388608]{0:T(1024)(128)(4,1)} %bitcast.68), calls=%async_computation.15 | async-start | bytes 8388608
  292.7 28.7 %slice-start.10 = ((s8[8388608]{0:T(1024)(128)(4,1)}), s8[4194304]{0:T(1024)(128)(4,1)S(1)}, s32[]{:S(2)}) async-start(s8[8388608]{0:T(1024)(128)(4,1)} %bitcast.70), calls=%async_computation.16 | async-start | bytes 8388608
  307.0 14.5 %slice-start.11 = ((s8[8388608]{0:T(1024)(128)(4,1)}), s8[4194304]{0:T(1024)(128)(4,1)S(1)}, s32[]{:S(2)}) async-start(s8[8388608]{0:T(1024)(128)(4,1)} %bitcast.70), calls=%async_computation.17 | async-start | bytes 8388608
  307.0 28.7 %slice-start.12 = ((s8[8388608]{0:T(1024)(128)(4,1)}), s8[4194304]{0:T(1024)(128)(4,1)S(1)}, s32[]{:S(2)}) async-start(s8[8388608]{0:T(1024)(128)(4,1)} %bitcast.72), calls=%async_computation.18 | async-start | bytes 8388608
  321.5 14.2 %slice-start.13 = ((s8[8388608]{0:T(1024)(128)(4,1)}), s8[4194304]{0:T(1024)(128)(4,1)S(1)}, s32[]{:S(2)}) async-start(s8[8388608]{0:T(1024)(128)(4,1)} %bitcast.72), calls=%async_computation.19 | async-start | bytes 8388608
  321.5 28.5 %slice-start.14 = ((s8[8388608]{0:T(1024)(128)(4,1)}), s8[4194304]{0:T(1024)(128)(4,1)S(1)}, s32[]{:S(2)}) async-start(s8[8388608]{0:T(1024)(128)(4,1)} %bitcast.74), calls=%async_computation.20 | async-start | bytes 8388608
  335.7 14.3 %slice-start.15 = ((s8[8388608]{0:T(1024)(128)(4,1)}), s8[4194304]{0:T(1024)(128)(4,1)S(1)}, s32[]{:S(2)}) async-start(s8[8388608]{0:T(1024)(128)(4,1)} %bitcast.74), calls=%async_computation.21 | async-start | bytes 8388608
  335.7 28.7 %slice-start = ((s8[8388608]{0:T(1024)(128)(4,1)}), s8[4194304]{0:T(1024)(128)(4,1)S(1)}, s32[]{:S(2)}) async-start(s8[8388608]{0:T(1024)(128)(4,1)} %bitcast.60), calls=%async_computation.6 | async-start | bytes 8388608
  350.0 14.5 %slice-start.1 = ((s8[8388608]{0:T(1024)(128)(4,1)}), s8[4194304]{0:T(1024)(128)(4,1)S(1)}, s32[]{:S(2)}) async-start(s8[8388608]{0:T(1024)(128)(4,1)} %bitcast.60), calls=%async_computation.7 | async-start | bytes 8388608
  350.0 28.4 %slice-start.18 = ((s8[8388608]{0:T(1024)(128)(4,1)}), s8[4194304]{0:T(1024)(128)(4,1)S(1)}, s32[]{:S(2)}) async-start(s8[8388608]{0:T(1024)(128)(4,1)} %bitcast.78), calls=%async_computation.24 | async-start | bytes 8388608
  364.5 13.9 %slice-start.19 = ((s8[8388608]{0:T(1024)(128)(4,1)}), s8[4194304]{0:T(1024)(128)(4,1)S(1)}, s32[]{:S(2)}) async-start(s8[8388608]{0:T(1024)(128)(4,1)} %bitcast.78), calls=%async_computation.25 | async-start | bytes 8388608
Sparse Core Ops, SparseCore 0:
  111.2 25.5 reduce-scatter.2
  140.8 69.2 all-reduce.2
  212.4 31.4 all-reduce.4
  397.3 148.0 reduce-scatter.4
